TPU v7x, 256 devices: a whole 4x4x8 slice. The times are simulated.
256 devices in a mesh: row: 8 (over x, core), col: 32 (over y, z).
Axes of the slice: x: 4, y: 4, z: 8, core: 2. Of those that a mesh axis runs over, the one named last changes fastest.
Arguments:
- grid_points: int32 [2, 6, 4096], P(None, None, 'row'), may hold values from 0 to 127
- variable: int32 [6, 4096], P(None, 'row'), may hold values from 0 to 2
Outputs:
- panel_factor: float32 [6, 4096, 1536], P(None, ('row', 'col'))
- trailing: float32 [6, 4096, 16384], P(None, 'row', 'col')
All inputs are finite; a program needn't handle non-finite values.
Results may differ from a plain program's by a relative error of at most 0.0042.
Values may be sent and summed in bfloat16 or wider, within the bound.
A program may use at most 128 MiB of HBM per device.

v0:
```python
import jax
import jax.numpy as jnp
from jax import lax
from jax.sharding import PartitionSpec as P

PANELS = 3
GRID = 128
range_scale = 0.05
nugget = 0.5
rho_first = 0.35
rho_second = 0.2
rho_third = 0.3
highest = lax.Precision.HIGHEST


def rows_first(arrays, axis, dims):
    turned = [jnp.moveaxis(a, dim, 0) for a, dim in zip(arrays, dims)]
    widths = [t[0].size for t in turned]
    both = jnp.concatenate([t.reshape(-1, w) for t, w in zip(turned, widths)], axis=1)
    whole = lax.all_gather(both, axis, axis=0, tiled=True)
    parts = jnp.split(whole, [sum(widths[:k]) for k in range(1, len(widths))], axis=1)
    return tuple(
        (
            jnp.moveaxis(b.reshape(-1, *t.shape[1:]), 0, dim)
            for b, t, dim in zip(parts, turned, dims)
        )
    )


def kind_scale(kinds):
    return jnp.where(kinds == 0, 1.0, jnp.where(kinds == 1, 1.3, 0.8))


def covariance(row_x, row_y, row_kind, col_x, col_y, col_kind):
    delta_x = (row_x[:, None] - col_x[None, :]).astype(jnp.float32)
    delta_y = (row_y[:, None] - col_y[None, :]).astype(jnp.float32)
    distance = jnp.sqrt(delta_x * delta_x + delta_y * delta_y) * (1.0 / (GRID * range_scale))
    order_sum = row_kind[:, None] + col_kind[None, :]
    dist_square = distance * distance
    dist_cube = dist_square * distance
    dist_fourth = dist_square * dist_square
    polynomial = jnp.where(order_sum == 0, 1.0, 1.0 + distance)
    polynomial = jnp.where(order_sum == 2, 1.0 + distance + dist_square / 3.0, polynomial)
    polynomial = jnp.where(
        order_sum == 3, 1.0 + distance + 0.4 * dist_square + dist_cube / 15.0, polynomial
    )
    polynomial = jnp.where(
        order_sum == 4,
        1.0 + distance + dist_square * (3.0 / 7.0) + dist_cube * (2.0 / 21.0) + dist_fourth / 105.0,
        polynomial,
    )
    correlation = jnp.where(
        row_kind[:, None] == col_kind[None, :],
        1.0,
        jnp.where(order_sum == 1, rho_first, jnp.where(order_sum == 2, rho_second, rho_third)),
    )
    scale_row = kind_scale(row_kind)
    scale_col = kind_scale(col_kind)
    return correlation * scale_row[:, None] * scale_col[None, :] * polynomial * jnp.exp(-distance)


def leading_factor(matrix, count, size):
    remaining = matrix
    lower_blocks = {}
    inverse_blocks = {}
    identity = jnp.eye(size, dtype=jnp.float32)
    for panel_step in range(count):
        row_begin = panel_step * size
        row_end = row_begin + size
        diag_factor = jnp.linalg.cholesky(remaining[row_begin:row_end, row_begin:row_end])
        diag_inverse = lax.linalg.triangular_solve(
            diag_factor, identity, left_side=True, lower=True
        )
        lower_blocks[panel_step, panel_step] = diag_factor
        inverse_blocks[panel_step, panel_step] = diag_inverse
        if panel_step + 1 < count:
            below_rows = jnp.dot(
                remaining[row_end:, row_begin:row_end], diag_inverse.T, precision=highest
            )
            for row_block in range(panel_step + 1, count):
                lower_blocks[row_block, panel_step] = below_rows[
                    (row_block - panel_step - 1) * size : (row_block - panel_step) * size
                ]
            trailing_part = remaining[row_end:, row_end:] - jnp.dot(
                below_rows, below_rows.T, precision=highest
            )
            remaining = remaining.at[row_end:, row_end:].set(trailing_part)
    for row_block in range(count):
        for col_block in range(row_block):
            running = jnp.zeros((size, size), jnp.float32)
            for mid_block in range(col_block, row_block):
                running = running + jnp.dot(
                    lower_blocks[row_block, mid_block],
                    inverse_blocks[mid_block, col_block],
                    precision=highest,
                )
            inverse_blocks[row_block, col_block] = -jnp.dot(
                inverse_blocks[row_block, row_block], running, precision=highest
            )
    zeros_block = jnp.zeros((size, size), jnp.float32)
    lower_rows = []
    inverse_rows = []
    for row_block in range(count):
        lower_rows.append(
            jnp.concatenate(
                [
                    lower_blocks[row_block, col_block] if col_block <= row_block else zeros_block
                    for col_block in range(count)
                ],
                1,
            )
        )
        inverse_rows.append(
            jnp.concatenate(
                [
                    inverse_blocks[row_block, col_block] if col_block <= row_block else zeros_block
                    for col_block in range(count)
                ],
                1,
            )
        )
    return (jnp.concatenate(lower_rows, 0), jnp.concatenate(inverse_rows, 0))


def local(grid_points, variable):
    rows_dev = variable.shape[0]
    tile_size = variable.shape[1]
    row_count = lax.axis_size("row")
    col_count = lax.axis_size("col")
    piece_rows = tile_size // col_count
    row_index = lax.axis_index("row")
    col_index = lax.axis_index("col")
    lead_size = PANELS * tile_size
    all_grid, all_kind = rows_first((grid_points, variable), "row", (2, 1))
    coord_x = all_grid[0].reshape(-1)
    coord_y = all_grid[1].reshape(-1)
    kinds = all_kind.reshape(-1)
    lead_x = coord_x[:lead_size]
    lead_y = coord_y[:lead_size]
    lead_kind = kinds[:lead_size]
    lead_cov = covariance(lead_x, lead_y, lead_kind, lead_x, lead_y, lead_kind)
    lead_cov = lead_cov + nugget * jnp.eye(lead_size, dtype=jnp.float32)
    lower_factor, inverse = leading_factor(lead_cov, PANELS, tile_size)
    offset = col_index * piece_rows
    mine_grid = lax.dynamic_slice_in_dim(grid_points, offset, piece_rows, 2)
    mine_kind = lax.dynamic_slice_in_dim(variable, offset, piece_rows, 1)
    piece_cov = covariance(
        mine_grid[0].reshape(-1),
        mine_grid[1].reshape(-1),
        mine_kind.reshape(-1),
        lead_x,
        lead_y,
        lead_kind,
    )
    solved = jnp.dot(piece_cov, inverse.T, precision=highest).reshape(
        rows_dev, piece_rows, lead_size
    )
    lead_rows = lax.dynamic_slice_in_dim(
        lower_factor,
        jnp.minimum(row_index * tile_size + offset, lead_size - piece_rows),
        piece_rows,
        0,
    )
    first_slot = jnp.where(row_index < PANELS, lead_rows, solved[0])
    panel_full = jnp.concatenate([first_slot[None], solved[1:]], 0)
    panel_half = panel_full.astype(jnp.bfloat16)
    target = PANELS + col_index
    col_start = target * tile_size
    col_x = lax.dynamic_slice_in_dim(coord_x, col_start, tile_size)
    col_y = lax.dynamic_slice_in_dim(coord_y, col_start, tile_size)
    col_kind = lax.dynamic_slice_in_dim(kinds, col_start, tile_size)
    row_iota = lax.broadcasted_iota(jnp.int32, (tile_size, tile_size), 0)
    col_iota = lax.broadcasted_iota(jnp.int32, (tile_size, tile_size), 1)

    def assemble(slot):
        cov_block = covariance(
            grid_points[0][slot], grid_points[1][slot], variable[slot], col_x, col_y, col_kind
        )
        equal = (slot * row_count + row_index == target) & (row_iota == col_iota)
        return jnp.where(equal, cov_block + nugget, cov_block)

    cov_tiles = lax.map(assemble, jnp.arange(rows_dev, dtype=jnp.int32))
    target_cov = covariance(col_x, col_y, col_kind, lead_x, lead_y, lead_kind)
    column_rows = jnp.dot(target_cov, inverse.T, precision=highest).astype(jnp.bfloat16)
    update = jnp.einsum(
        "sik,jk->sij",
        lax.all_gather(panel_half, "col", axis=1, tiled=True),
        column_rows,
        preferred_element_type=jnp.float32,
    )
    return (panel_full, cov_tiles - update)


def solution(mesh):
    return jax.shard_map(
        local,
        mesh=mesh,
        in_specs=(P(None, None, "row"), P(None, "row")),
        out_specs=(P(None, ("row", "col"), None), P(None, "row", "col")),
        check_vma=False,
    )
```

profile of v0, /device:TPU:1, one launch (start us, length us, event | category | flops | bytes accessed | tf_op | source)
XLA Modules:
  0.0 741.4 jit_solution(12981079836239768969)
XLA Ops:
  8.7 16.0 %all_gather.6 = s32[4096,18]{0,1:T(8,128)S(1)} all-gather(s32[512,18]{0,1:T(8,128)S(1)} %pad_add_fusion), channel_id=1, replica_groups=mesh['row'=8,'col'=32] {'row'}, dimensions={0}, use_global_device_ids=true | all-gather | bytes 331776 | tf_op jit(solution)/shard_map/all_gather | solution.py:20
  25.8 18.3 %fusion.28 = f32[1536,1536]{0,1:T(8,128)S(1)} fusion(s32[1536]{0:T(1024)S(1)} %slice.297, s32[1536]{0:T(1024)S(1)} %slice.295, f32[1536]{0:T(1024)S(1)} %select_select_fusion.5, s32[1536]{0:T(1024)S(1)} %slice.293), kind=kLoop, calls=%fused_computation.64 | loop fusion | flops 108527616 | bytes 9461760 | tf_op jit(solution)/shard_map/add | solution.py:142
  44.2 3.6 copy-done
  49.7 11.7 %cholesky.374 = f32[128,128]{1,0:T(8,128)S(1)} custom-call(f32[128,128]{1,0:T(8,128)S(1)} %cholesky.586), custom_call_target="Cholesky" | custom-call | tf_op jit(solution)/shard_map/jit(cholesky)/cholesky | solution.py:70
  61.5 9.8 %custom-call.31 = f32[1,128,128]{1,2,0:T(8,128)S(1)} custom-call(f32[1,128,128]{2,1,0:T(8,128)S(1)} %get-tuple-element.310), custom_call_target="InvertDiagBlocksLowerTriangular" | custom-call | tf_op jit(solution)/shard_map/jit(cholesky)/cholesky | solution.py:70
  72.1 11.7 %cholesky.393 = f32[128,128]{1,0:T(8,128)S(1)} custom-call(f32[128,128]{1,0:T(8,128)S(1)} %cholesky.590), custom_call_target="Cholesky" | custom-call | tf_op jit(solution)/shard_map/jit(cholesky)/cholesky | solution.py:70
  83.8 10.2 %custom-call.32 = f32[1,128,128]{1,2,0:T(8,128)S(1)} custom-call(f32[1,128,128]{2,1,0:T(8,128)S(1)} %get-tuple-element.307), custom_call_target="InvertDiagBlocksLowerTriangular" | custom-call | tf_op jit(solution)/shard_map/jit(cholesky)/cholesky | solution.py:70
  94.7 11.7 %cholesky.414 = f32[128,128]{1,0:T(8,128)S(1)} custom-call(f32[128,128]{1,0:T(8,128)S(1)} %cholesky.595), custom_call_target="Cholesky" | custom-call | tf_op jit(solution)/shard_map/jit(cholesky)/cholesky | solution.py:70
  107.1 9.8 %custom-call.33 = f32[1,128,128]{1,2,0:T(8,128)S(1)} custom-call(f32[1,128,128]{2,1,0:T(8,128)S(1)} %get-tuple-element.304), custom_call_target="InvertDiagBlocksLowerTriangular" | custom-call | tf_op jit(solution)/shard_map/jit(cholesky)/cholesky | solution.py:70
  117.5 11.7 %cholesky.431 = f32[128,128]{1,0:T(8,128)S(1)} custom-call(f32[128,128]{1,0:T(8,128)S(1)} %convolution_subtract_fusion.19), custom_call_target="Cholesky" | custom-call | tf_op jit(solution)/shard_map/jit(cholesky)/cholesky | solution.py:70
  134.6 7.9 %while.22 = (s32[]{:T(128)}, f32[512,512]{1,0:T(8,128)S(1)}, s32[4,2]{0,1:T(2,128)S(1)}, f32[4,128,128]{2,1,0:T(8,128)S(1)}, s32[]{:T(128)}) while((s32[]{:T(128)}, f32[512,512]{1,0:T(8,128)S(1)}, s32[4,2]{0,1:T(2,128)S(1)}, f32[4,128,128]{2,1,0:T(8,128)S(1)}, s32[]{:T(128)}) %tuple.122), condition=%wide.while_cond.2, body=%wide.while_body.2.sunk | while | flops 2 | bytes 131181 | solution.py:71
  142.5 39.3 %custom-call.34 = f32[4,128,128]{1,2,0:T(8,128)S(1)} custom-call(f32[4,128,128]{2,1,0:T(8,128)S(1)} %get-tuple-element.206), custom_call_target="InvertDiagBlocksLowerTriangular" | custom-call | tf_op jit(solution)/shard_map/triangular_solve/custom-call.3 | solution.py:71
  185.0 5.2 fusion.82
  193.1 9.2 %slice_subtract_fusion = f32[1024,1024]{0,1:T(8,128)S(1)} fusion(f32[1536,1536]{0,1:T(8,128)} %copy-done, f32[1024,512]{0,1:T(8,128)S(1)} %fusion.82), kind=kOutput, calls=%fused_computation.90 | convolution fusion | flops 6443499520 | bytes 12582912 | tf_op jit(solution)/shard_map/dot_general | solution.py:84
  210.8 11.7 %cholesky.446 = f32[128,128]{1,0:T(8,128)S(1)} custom-call(f32[128,128]{1,0:T(8,128)S(1)} %cholesky.599), custom_call_target="Cholesky" | custom-call | tf_op jit(solution)/shard_map/jit(cholesky)/cholesky | solution.py:70
  223.2 10.6 %custom-call.35 = f32[1,128,128]{1,2,0:T(8,128)S(1)} custom-call(f32[1,128,128]{2,1,0:T(8,128)} %get-tuple-element.300), custom_call_target="InvertDiagBlocksLowerTriangular" | custom-call | tf_op jit(solution)/shard_map/jit(cholesky)/cholesky | solution.py:70
  239.8 3.9 fusion.312
  245.7 11.9 %cholesky.465 = f32[128,128]{1,0:T(8,128)S(1)} custom-call(f32[128,128]{1,0:T(8,128)S(1)} %cholesky.603), custom_call_target="Cholesky" | custom-call | tf_op jit(solution)/shard_map/jit(cholesky)/cholesky | solution.py:70
  261.1 9.8 %custom-call.36 = f32[1,128,128]{1,2,0:T(8,128)S(1)} custom-call(f32[1,128,128]{2,1,0:T(8,128)S(1)} %get-tuple-element.297), custom_call_target="InvertDiagBlocksLowerTriangular" | custom-call | tf_op jit(solution)/shard_map/jit(cholesky)/cholesky | solution.py:70
  274.2 11.7 %cholesky.486 = f32[128,128]{1,0:T(8,128)S(1)} custom-call(f32[128,128]{1,0:T(8,128)S(1)} %cholesky.608), custom_call_target="Cholesky" | custom-call | tf_op jit(solution)/shard_map/jit(cholesky)/cholesky | solution.py:70
  287.3 9.8 %custom-call.37 = f32[1,128,128]{1,2,0:T(8,128)S(1)} custom-call(f32[1,128,128]{2,1,0:T(8,128)S(1)} %get-tuple-element.294), custom_call_target="InvertDiagBlocksLowerTriangular" | custom-call | tf_op jit(solution)/shard_map/jit(cholesky)/cholesky | solution.py:70
  299.4 12.1 %cholesky.503 = f32[128,128]{1,0:T(8,128)S(1)} custom-call(f32[128,128]{1,0:T(8,128)S(1)} %convolution_subtract_fusion.18), custom_call_target="Cholesky" | custom-call | tf_op jit(solution)/shard_map/jit(cholesky)/cholesky | solution.py:70
  318.3 10.8 %while.23 = (s32[]{:T(128)}, f32[512,512]{1,0:T(8,128)}, s32[4,2]{0,1:T(2,128)S(1)}, f32[4,128,128]{2,1,0:T(8,128)S(1)}, s32[]{:T(128)}) while((s32[]{:T(128)}, f32[512,512]{1,0:T(8,128)}, s32[4,2]{0,1:T(2,128)S(1)}, f32[4,128,128]{2,1,0:T(8,128)S(1)}, s32[]{:T(128)}) %tuple.137), condition=%wide.while_cond.2.clone, body=%wide.while_body.2.clone.sunk | while | flops 2 | bytes 131181 | solution.py:71
  329.1 39.9 %custom-call.38 = f32[4,128,128]{1,2,0:T(8,128)} custom-call(f32[4,128,128]{2,1,0:T(8,128)S(1)} %get-tuple-element.207), custom_call_target="InvertDiagBlocksLowerTriangular" | custom-call | tf_op jit(solution)/shard_map/triangular_solve/custom-call.3 | solution.py:71
  378.5 3.2 fusion.108
  381.7 4.2 convolution_subtract_fusion.1
  391.2 11.7 %cholesky.518 = f32[128,128]{1,0:T(8,128)S(1)} custom-call(f32[128,128]{1,0:T(8,128)S(1)} %cholesky.612), custom_call_target="Cholesky" | custom-call | tf_op jit(solution)/shard_map/jit(cholesky)/cholesky | solution.py:70
  403.6 10.8 %custom-call.39 = f32[1,128,128]{1,2,0:T(8,128)S(1)} custom-call(f32[1,128,128]{2,1,0:T(8,128)} %get-tuple-element.290), custom_call_target="InvertDiagBlocksLowerTriangular" | custom-call | tf_op jit(solution)/shard_map/jit(cholesky)/cholesky | solution.py:70
  420.3 4.0 fusion.223
  429.4 4.4 convolution_negate_fusion.2
  433.9 11.7 %cholesky.537 = f32[128,128]{1,0:T(8,128)S(1)} custom-call(f32[128,128]{1,0:T(8,128)S(1)} %slice-done), custom_call_target="Cholesky" | custom-call | tf_op jit(solution)/shard_map/jit(cholesky)/cholesky | solution.py:70
  447.9 10.0 %custom-call.40 = f32[1,128,128]{1,2,0:T(8,128)S(1)} custom-call(f32[1,128,128]{2,1,0:T(8,128)S(1)} %get-tuple-element.287), custom_call_target="InvertDiagBlocksLowerTriangular" | custom-call | tf_op jit(solution)/shard_map/jit(cholesky)/cholesky | solution.py:70
  461.0 13.2 %cholesky.558 = f32[128,128]{1,0:T(8,128)} custom-call(f32[128,128]{1,0:T(8,128)} %cholesky.621), custom_call_target="Cholesky" | custom-call | tf_op jit(solution)/shard_map/jit(cholesky)/cholesky | solution.py:70
  476.3 11.3 %custom-call.41 = f32[1,128,128]{1,2,0:T(8,128)} custom-call(f32[1,128,128]{2,1,0:T(8,128)} %get-tuple-element.284), custom_call_target="InvertDiagBlocksLowerTriangular" | custom-call | tf_op jit(solution)/shard_map/jit(cholesky)/cholesky | solution.py:70
  489.9 11.7 %cholesky.575 = f32[128,128]{1,0:T(8,128)S(1)} custom-call(f32[128,128]{1,0:T(8,128)S(1)} %convolution_subtract_fusion.17), custom_call_target="Cholesky" | custom-call | tf_op jit(solution)/shard_map/jit(cholesky)/cholesky | solution.py:70
  506.3 12.0 %while.24 = (s32[]{:T(128)}, f32[512,512]{1,0:T(8,128)}, s32[4,2]{0,1:T(2,128)S(1)}, f32[4,128,128]{2,1,0:T(8,128)S(1)}, s32[]{:T(128)}) while((s32[]{:T(128)}, f32[512,512]{1,0:T(8,128)}, s32[4,2]{0,1:T(2,128)S(1)}, f32[4,128,128]{2,1,0:T(8,128)S(1)}, s32[]{:T(128)}) %tuple.138), condition=%wide.while_cond.2.clone.1, body=%wide.while_body.2.clone.1.sunk | while | flops 2 | bytes 131181 | solution.py:71
  518.3 39.7 %custom-call.42 = f32[4,128,128]{1,2,0:T(8,128)S(1)} custom-call(f32[4,128,128]{2,1,0:T(8,128)S(1)} %get-tuple-element.208), custom_call_target="InvertDiagBlocksLowerTriangular" | custom-call | tf_op jit(solution)/shard_map/triangular_solve/custom-call.3 | solution.py:71
  565.8 3.4 convolution_add_fusion
  581.3 20.2 %fusion.38 = f32[1536,1536]{1,0:T(8,128)} fusion(f32[512,512]{1,0:T(8,128)S(1)} %cholesky.441, f32[512,512]{1,0:T(8,128)} %pad_maximum_fusion.1, f32[128,512]{1,0:T(8,128)S(1)} %fusion.240, f32[128,512]{1,0:T(8,128)} %copy-done.12, f32[128,512]{1,0:T(8,128)S(1)} %fusion.243, f32[128,512]{1,0:T(8,128)S(1)} %fusion.205, f32[512,512]{1,0:T(8,128)} %convolution_negate_fusion, ...), kind=kLoop, calls=%fused_computation.76 | loop fusion | flops 33030144 | bytes 16777216 | tf_op jit(solution)/shard_map/concatenate | solution.py:122
  601.6 13.2 %fusion.140 = f32[96,1536]{1,0:T(8,128)S(1)} fusion(f32[1536,1536]{1,0:T(8,128)} %fusion.38, s32[1536]{0:T(1024)S(1)} %copy-done.28, s32[96]{0:T(128)S(1)} %sub.151, s32[1536]{0:T(1024)S(1)} %copy-done.26, s32[96]{0:T(128)S(1)} %sub.147, f32[1536]{0:T(1024)S(1)} %select_select_fusion.5, f32[96]{0:T(128)S(1)} %compare_select_fusion.1, ...), kind=kOutput, calls=%fused_computation.241 | convolution fusion | flops 2724249600 | bytes 10053120 | tf_op jit(solution)/shard_map/dot_general | solution.py:155
  621.8 28.3 %fusion.79 = bf16[512,1536,1]{1,0,2:T(8,128)(2,1)S(1)} fusion(f32[1536,1536]{1,0:T(8,128)} %fusion.38, s32[1536]{0:T(1024)S(1)} %copy-done.28, s32[512]{0:T(512)S(1)} %dynamic_slice.42, s32[1536]{0:T(1024)S(1)} %copy-done.26, s32[512]{0:T(512)S(1)} %dynamic_slice.41, f32[1536]{0:T(1024)S(1)} %select_select_fusion.5, f32[512]{0:T(512)S(1)} %get-tuple-element.255, ...), kind=kOutput, calls=%fused_computation.131 | convolution fusion | flops 14530117632 | bytes 11042816 | tf_op jit(solution)/shard_map/dot_general | solution.py:184
  650.1 42.0 %while.21 = (s32[]{:T(128)}, f32[6,512,512]{2,1,0:T(8,128)}, s32[6]{0:T(128)S(1)}, s32[]{:T(128)}, s32[]{:T(128)}, /*index=5*/s32[6,512]{1,0:T(8,128)}, s32[512]...) while((s32[]{:T(128)}, f32[6,512,512]{2,1,0:T(8,128)}, ...), condition=%wide.region_9.12_spmd.clone, body=%wide.region_8.11_spmd.clone.sunk | while | flops 12324872 | bytes 1135325 | solution.py:182
  654.3 3.0 fusion.358
  661.2 3.0 fusion.358
  668.2 3.0 fusion.358
  689.0 3.0 fusion.358
  692.0 30.6 %all-gather.2.cloned.1.call-done = bf16[6,512,1536]{2,1,0:T(8,128)(2,1)} async-done(((bf16[6,16,1536]{2,1,0:T(8,128)(2,1)}), bf16[6,512,1536]{2,1,0:T(8,128)(2,1)}) %all-gather.2.cloned.1.call-update) | async-done | bytes 9437200 | tf_op jit(solution)/shard_map/all_gather | solution.py:187
  722.6 11.6 %convolution_subtract_fusion = f32[6,512,512]{2,1,0:T(8,128)} fusion(f32[6,512,512]{2,1,0:T(8,128)} %get-tuple-element.163, bf16[6,512,1536]{2,1,0:T(8,128)(2,1)} %all-gather.2.cloned.1.call-done, bf16[512,1536,1]{1,0,2:T(8,128)(2,1)S(1)} %fusion.79), kind=kOutput, calls=%fused_computation.132 | convolution fusion | flops 4833411072 | bytes 23592960 | tf_op jit(solution)/shard_map/sik,jk->sij/dot_general | solution.py:185
  (264 shorter events, 157.8 us)
Async XLA Ops:
  7.2 715.5 %all-gather.2.cloned.1.call-start = ((), (), s32[]{:S(2)}) async-start(), calls=%async_computation | async-start | bytes 9732096 | tf_op jit(solution)/shard_map/all_gather | solution.py:187
  24.8 0.6 copy-start.22
  25.4 18.7 %copy-start.23 = (s32[1536]{0:T(1024)}, s32[1536]{0:T(1024)S(1)}, u32[]{:S(2)}) copy-start(s32[1536]{0:T(1024)S(1)} %slice.293) | copy-start | bytes 18436
  25.6 349.9 %copy-start.2 = (f32[512,512]{1,0:T(8,128)}, f32[512,512]{1,0:T(8,128)S(1)}, u32[]{:S(2)}) copy-start(f32[512,512]{1,0:T(8,128)S(1)} %fusion.116) | copy-start | bytes 3145732
  25.7 18.5 %copy-start.29 = (s32[24576]{0:T(1024)}, s32[24576]{0:T(1024)S(1)}, u32[]{:S(2)}) copy-start(s32[24576]{0:T(1024)S(1)} %reshape_squeeze.6) | copy-start | bytes 294916
  25.7 18.5 %copy-start.25 = (s32[1536]{0:T(1024)}, s32[1536]{0:T(1024)S(1)}, u32[]{:S(2)}) copy-start(s32[1536]{0:T(1024)S(1)} %slice.295) | copy-start | bytes 18436
  25.8 18.4 %copy-start.30 = (s32[24576]{0:T(1024)}, s32[24576]{0:T(1024)S(1)}, u32[]{:S(2)}) copy-start(s32[24576]{0:T(1024)S(1)} %reshape_squeeze.7) | copy-start | bytes 294916
  25.8 18.4 %copy-start.27 = (s32[1536]{0:T(1024)}, s32[1536]{0:T(1024)S(1)}, u32[]{:S(2)}) copy-start(s32[1536]{0:T(1024)S(1)} %slice.297) | copy-start | bytes 18436
  44.2 3.6 copy-start
  182.3 57.6 %copy-start.4 = (f32[128,512]{1,0:T(8,128)}, f32[128,512]{1,0:T(8,128)S(1)}, u32[]{:S(2)}) copy-start(f32[128,512]{1,0:T(8,128)S(1)} %fusion.209) | copy-start | bytes 786436
  183.1 7.2 copy-start.7
  183.9 6.3 copy-start.10
  185.0 5.3 copy-start.13
  202.3 2.0 copy-start.1
  209.8 1.1 copy-start.18
  372.8 5.7 copy-start.5
  375.5 6.2 copy-start.8
  378.5 3.2 copy-start.11
  390.2 1.0 copy-start.17
  420.3 13.6 %slice-start = ((f32[384,128]{1,0:T(8,128)}), f32[128,128]{1,0:T(8,128)S(1)}, s32[]{:S(2)}) async-start(f32[384,128]{1,0:T(8,128)} %convolution_subtract_fusion.11), calls=%async_computation.1 | async-start | bytes 131072 | tf_op jit(solution)/shard_map/jit(cholesky)/cholesky | solution.py:70
  429.4 128.6 %copy-start.3 = (f32[512,512]{1,0:T(8,128)S(1)}, f32[512,512]{1,0:T(8,128)}, u32[]{:S(2)}) copy-start(f32[512,512]{1,0:T(8,128)} %copy-done.2) | copy-start | bytes 3145732
  506.3 69.4 %copy-start.20 = (s32[2,6,512]{2,0,1:T(2,128)S(1)}, s32[2,6,512]{2,0,1:T(2,128)}, u32[]{:S(2)}) copy-start(s32[2,6,512]{2,0,1:T(2,128)} %param.11) | copy-start | bytes 73732
  558.1 2.1 copy-start.21
  558.1 14.0 %copy-start.14 = (f32[512,512]{1,0:T(8,128)S(1)}, f32[512,512]{1,0:T(8,128)}, u32[]{:S(2)}) copy-start(f32[512,512]{1,0:T(8,128)} %fusion.223) | copy-start | bytes 3145732
  561.5 19.8 %copy-start.6 = (f32[128,512]{1,0:T(8,128)S(1)}, f32[128,512]{1,0:T(8,128)}, u32[]{:S(2)}) copy-start(f32[128,512]{1,0:T(8,128)} %copy-done.5) | copy-start | bytes 786436
  561.5 19.8 %copy-start.9 = (f32[128,512]{1,0:T(8,128)S(1)}, f32[128,512]{1,0:T(8,128)}, u32[]{:S(2)}) copy-start(f32[128,512]{1,0:T(8,128)} %copy-done.8) | copy-start | bytes 786436
  562.9 9.2 %copy-start.12 = (f32[128,512]{1,0:T(8,128)}, f32[128,512]{1,0:T(8,128)S(1)}, u32[]{:S(2)}) copy-start(f32[128,512]{1,0:T(8,128)S(1)} %fusion.241) | copy-start | bytes 786436
  581.2 20.4 %copy-start.24 = (s32[1536]{0:T(1024)S(1)}, s32[1536]{0:T(1024)}, u32[]{:S(2)}) copy-start(s32[1536]{0:T(1024)} %copy-done.23) | copy-start | bytes 18436
  581.2 20.4 %copy-start.26 = (s32[1536]{0:T(1024)S(1)}, s32[1536]{0:T(1024)}, u32[]{:S(2)}) copy-start(s32[1536]{0:T(1024)} %copy-done.25) | copy-start | bytes 18436
  581.2 20.4 %copy-start.28 = (s32[1536]{0:T(1024)S(1)}, s32[1536]{0:T(1024)}, u32[]{:S(2)}) copy-start(s32[1536]{0:T(1024)} %copy-done.27) | copy-start | bytes 18436
  601.5 14.9 %copy-start.15 = (f32[512,512]{1,0:T(8,128)S(1)}, f32[512,512]{1,0:T(8,128)}, u32[]{:S(2)}) copy-start(f32[512,512]{1,0:T(8,128)} %get-tuple-element.264) | copy-start | bytes 3145732
  601.6 14.9 %copy-start.16 = (f32[512,512]{1,0:T(8,128)S(1)}, f32[512,512]{1,0:T(8,128)}, u32[]{:S(2)}) copy-start(f32[512,512]{1,0:T(8,128)} %get-tuple-element.262) | copy-start | bytes 3145732
  614.8 0.8 copy-start.19
Sparse Core Ops, SparseCore 0:
  619.6 102.9 all-gather.1
where the time goes:
time: 750 us; the launch traced here: 741 us
  other arithmetic  440 us (59%)
  matrix products  140 us (19%)
  local copies, waits for them, and re-layouts  76.1 us (10%)
  waiting for transfers between devices  30.6 us (4%)
  between operations  22.7 us (3%)
  blocking collectives  16 us (2%)
  loops' own time  15.8 us (2%)
    another operation x44, other arithmetic, leading_factor(): jnp.linalg.cholesky(remaining[row_begin:row_end, row_begin:row_end])  247 us
    another operation x8, other arithmetic, leading_factor(): lax.linalg.triangular_solve(diag_factor, identity, left_side=True, lower=...  127 us
    another operation x40, local copies, waits for them, and re-layouts, leading_factor(): lax.linalg.triangular_solve(diag_factor, identity, left_side=True, lower=...  30.6 us
    all_gather x1, waiting for transfers between devices, local(): lax.all_gather(panel_half, 'col', axis=1, tiled=True)  30.6 us
    dot_general x1, matrix products, local(): jnp.dot(target_cov, inverse.T, precision=highest).astype(jnp.bfloat16)  28.3 us
    another operation x18, matrix products, leading_factor(): jnp.linalg.cholesky(remaining[row_begin:row_end, row_begin:row_end])  20.6 us
    concatenate x1, other arithmetic, leading_factor(): return (jnp.concatenate(lower_rows, 0), jnp.concatenate(inverse_rows, 0))  20.2 us
    another operation x21, matrix products, leading_factor(): lax.linalg.triangular_solve(diag_factor, identity, left_side=True, lower=...  20 us
  transfers between devices with their start and end apart: 1, of which 1 were waited for; matrix products, arithmetic and copies ran while one was open for 8% of the time, Pallas kernels for 0%

commit v1 on v0

--- a/solution.py
+++ b/solution.py
@@ -11,6 +11,11 @@
 rho_second = 0.2
 rho_third = 0.3
 highest = lax.Precision.HIGHEST
+
+
+def all_by_exchange(x, mesh_axis, dim):
+    sent = jnp.stack([x] * lax.axis_size(mesh_axis))
+    return jnp.concatenate(lax.all_to_all(sent, mesh_axis, 0, 0), axis=dim)
 
 
 def rows_first(arrays, axis, dims):
@@ -184,7 +189,7 @@
     column_rows = jnp.dot(target_cov, inverse.T, precision=highest).astype(jnp.bfloat16)
     update = jnp.einsum(
         "sik,jk->sij",
-        lax.all_gather(panel_half, "col", axis=1, tiled=True),
+        all_by_exchange(panel_half, "col", 1),
         column_rows,
         preferred_element_type=jnp.float32,
     )

time: 750 us -> 877 us (1.17)
  waiting for transfers between devices: 30.6 us -> 142 us
  local copies, waits for them, and re-layouts: 76.1 us -> 90.9 us
  between operations: 22.7 us -> 9.48 us
  starting transfers between devices: 0.04 us -> 10.2 us
    all_to_all x0 -> x1, waiting for transfers between devices: none -> 142 us  [all_by_exchange(): return jnp.concatenate(lax.all_to_all(sent, mesh_axis, 0, 0), axis=dim)]
    all_gather x1 -> x0, waiting for transfers between devices: 30.6 us -> none  [local(): lax.all_gather(panel_half, 'col', axis=1, tiled=True)]
    all_to_all x0 -> x1, starting transfers between devices: none -> 10.2 us  [all_by_exchange(): return jnp.concatenate(lax.all_to_all(sent, mesh_axis, 0, 0), axis=dim)]
  transfers between devices with their start and end apart: 1 -> 1, of which waited for: 1 -> 1; matrix products, arithmetic and copies ran while one was open for 8% -> 7% of each run, Pallas kernels for 0% -> 0%
where the time goes in v1:
time: 877 us; the launch traced here: 863 us
  other arithmetic  440 us (50%)
  waiting for transfers between devices  142 us (16%)
  matrix products  140 us (16%)
  local copies, waits for them, and re-layouts  90.9 us (10%)
  blocking collectives  16 us (2%)
  loops' own time  14.2 us (2%)
  starting transfers between devices  10.2 us (1%)
  between operations  9.48 us (1%)
    another operation x44, other arithmetic, leading_factor(): jnp.linalg.cholesky(remaining[row_begin:row_end, row_begin:row_end])  247 us
    all_to_all x1, waiting for transfers between devices, all_by_exchange(): return jnp.concatenate(lax.all_to_all(sent, mesh_axis, 0, 0), axis=dim)  142 us
    another operation x8, other arithmetic, leading_factor(): lax.linalg.triangular_solve(diag_factor, identity, left_side=True, lower=...  128 us
    another operation x40, local copies, waits for them, and re-layouts, leading_factor(): lax.linalg.triangular_solve(diag_factor, identity, left_side=True, lower=...  31.6 us
    dot_general x1, matrix products, local(): jnp.dot(target_cov, inverse.T, precision=highest).astype(jnp.bfloat16)  28.1 us
    another operation x18, matrix products, leading_factor(): jnp.linalg.cholesky(remaining[row_begin:row_end, row_begin:row_end])  21.5 us
    another operation x21, matrix products, leading_factor(): lax.linalg.triangular_solve(diag_factor, identity, left_side=True, lower=...  20 us
    concatenate x1, other arithmetic, leading_factor(): return (jnp.concatenate(lower_rows, 0), jnp.concatenate(inverse_rows, 0))  19.9 us
  transfers between devices with their start and end apart: 1, of which 1 were waited for; matrix products, arithmetic and copies ran while one was open for 7% of the time, Pallas kernels for 0%

profile of v1, /device:TPU:1, one launch (start us, length us, event | category | flops | bytes accessed | tf_op | source)
XLA Modules:
  0.0 862.7 jit_solution(14922558494883323160)
XLA Ops:
  2.1 16.0 %all_gather.3 = s32[4096,18]{0,1:T(8,128)S(1)} all-gather(s32[512,18]{0,1:T(8,128)S(1)} %pad_add_fusion), channel_id=1, replica_groups=mesh['row'=8,'col'=32] {'row'}, dimensions={0}, use_global_device_ids=true | all-gather | bytes 331776 | tf_op jit(solution)/shard_map/all_gather | solution.py:25
  20.0 18.3 %fusion.28 = f32[1536,1536]{0,1:T(8,128)S(1)} fusion(s32[1536]{0:T(1024)S(1)} %slice.297, s32[1536]{0:T(1024)S(1)} %slice.295, f32[1536]{0:T(1024)S(1)} %select_select_fusion.5, s32[1536]{0:T(1024)S(1)} %slice.293), kind=kLoop, calls=%fused_computation.64 | loop fusion | flops 108527616 | bytes 9461760 | tf_op jit(solution)/shard_map/add | solution.py:147
  38.4 3.6 copy-done
  43.9 11.7 %cholesky.374 = f32[128,128]{1,0:T(8,128)S(1)} custom-call(f32[128,128]{1,0:T(8,128)S(1)} %cholesky.586), custom_call_target="Cholesky" | custom-call | tf_op jit(solution)/shard_map/jit(cholesky)/cholesky | solution.py:75
  55.6 9.8 %custom-call.31 = f32[1,128,128]{1,2,0:T(8,128)S(1)} custom-call(f32[1,128,128]{2,1,0:T(8,128)S(1)} %get-tuple-element.310), custom_call_target="InvertDiagBlocksLowerTriangular" | custom-call | tf_op jit(solution)/shard_map/jit(cholesky)/cholesky | solution.py:75
  66.9 11.7 %cholesky.393 = f32[128,128]{1,0:T(8,128)S(1)} custom-call(f32[128,128]{1,0:T(8,128)S(1)} %cholesky.590), custom_call_target="Cholesky" | custom-call | tf_op jit(solution)/shard_map/jit(cholesky)/cholesky | solution.py:75
  78.7 10.2 %custom-call.32 = f32[1,128,128]{1,2,0:T(8,128)S(1)} custom-call(f32[1,128,128]{2,1,0:T(8,128)S(1)} %get-tuple-element.307), custom_call_target="InvertDiagBlocksLowerTriangular" | custom-call | tf_op jit(solution)/shard_map/jit(cholesky)/cholesky | solution.py:75
  90.4 11.7 %cholesky.414 = f32[128,128]{1,0:T(8,128)S(1)} custom-call(f32[128,128]{1,0:T(8,128)S(1)} %cholesky.595), custom_call_target="Cholesky" | custom-call | tf_op jit(solution)/shard_map/jit(cholesky)/cholesky | solution.py:75
  102.9 9.8 %custom-call.33 = f32[1,128,128]{1,2,0:T(8,128)S(1)} custom-call(f32[1,128,128]{2,1,0:T(8,128)S(1)} %get-tuple-element.304), custom_call_target="InvertDiagBlocksLowerTriangular" | custom-call | tf_op jit(solution)/shard_map/jit(cholesky)/cholesky | solution.py:75
  113.3 11.7 %cholesky.431 = f32[128,128]{1,0:T(8,128)S(1)} custom-call(f32[128,128]{1,0:T(8,128)S(1)} %convolution_subtract_fusion.19), custom_call_target="Cholesky" | custom-call | tf_op jit(solution)/shard_map/jit(cholesky)/cholesky | solution.py:75
  131.1 8.0 while.22
  139.1 39.3 %custom-call.34 = f32[4,128,128]{1,2,0:T(8,128)S(1)} custom-call(f32[4,128,128]{2,1,0:T(8,128)S(1)} %get-tuple-element.206), custom_call_target="InvertDiagBlocksLowerTriangular" | custom-call | tf_op jit(solution)/shard_map/triangular_solve/custom-call.3 | solution.py:76
  181.6 5.2 fusion.82
  189.8 9.2 %slice_subtract_fusion = f32[1024,1024]{0,1:T(8,128)S(1)} fusion(f32[1536,1536]{0,1:T(8,128)} %copy-done, f32[1024,512]{0,1:T(8,128)S(1)} %fusion.82), kind=kOutput, calls=%fused_computation.90 | convolution fusion | flops 6443499520 | bytes 12582912 | tf_op jit(solution)/shard_map/dot_general | solution.py:89
  207.4 11.7 %cholesky.446 = f32[128,128]{1,0:T(8,128)S(1)} custom-call(f32[128,128]{1,0:T(8,128)S(1)} %cholesky.599), custom_call_target="Cholesky" | custom-call | tf_op jit(solution)/shard_map/jit(cholesky)/cholesky | solution.py:75
  219.7 10.6 %custom-call.35 = f32[1,128,128]{1,2,0:T(8,128)S(1)} custom-call(f32[1,128,128]{2,1,0:T(8,128)} %get-tuple-element.300), custom_call_target="InvertDiagBlocksLowerTriangular" | custom-call | tf_op jit(solution)/shard_map/jit(cholesky)/cholesky | solution.py:75
  236.3 3.9 fusion.312
  242.2 11.9 %cholesky.465 = f32[128,128]{1,0:T(8,128)S(1)} custom-call(f32[128,128]{1,0:T(8,128)S(1)} %cholesky.603), custom_call_target="Cholesky" | custom-call | tf_op jit(solution)/shard_map/jit(cholesky)/cholesky | solution.py:75
  257.7 9.8 %custom-call.36 = f32[1,128,128]{1,2,0:T(8,128)S(1)} custom-call(f32[1,128,128]{2,1,0:T(8,128)S(1)} %get-tuple-element.297), custom_call_target="InvertDiagBlocksLowerTriangular" | custom-call | tf_op jit(solution)/shard_map/jit(cholesky)/cholesky | solution.py:75
  270.8 11.7 %cholesky.486 = f32[128,128]{1,0:T(8,128)S(1)} custom-call(f32[128,128]{1,0:T(8,128)S(1)} %cholesky.608), custom_call_target="Cholesky" | custom-call | tf_op jit(solution)/shard_map/jit(cholesky)/cholesky | solution.py:75
  283.9 9.8 %custom-call.37 = f32[1,128,128]{1,2,0:T(8,128)S(1)} custom-call(f32[1,128,128]{2,1,0:T(8,128)S(1)} %get-tuple-element.294), custom_call_target="InvertDiagBlocksLowerTriangular" | custom-call | tf_op jit(solution)/shard_map/jit(cholesky)/cholesky | solution.py:75
  296.0 12.1 %cholesky.503 = f32[128,128]{1,0:T(8,128)S(1)} custom-call(f32[128,128]{1,0:T(8,128)S(1)} %convolution_subtract_fusion.18), custom_call_target="Cholesky" | custom-call | tf_op jit(solution)/shard_map/jit(cholesky)/cholesky | solution.py:75
  314.7 12.0 %while.23 = (s32[]{:T(128)}, f32[512,512]{1,0:T(8,128)}, s32[4,2]{0,1:T(2,128)S(1)}, f32[4,128,128]{2,1,0:T(8,128)S(1)}, s32[]{:T(128)}) while((s32[]{:T(128)}, f32[512,512]{1,0:T(8,128)}, s32[4,2]{0,1:T(2,128)S(1)}, f32[4,128,128]{2,1,0:T(8,128)S(1)}, s32[]{:T(128)}) %tuple.135), condition=%wide.while_cond.2.clone, body=%wide.while_body.2.clone.sunk | while | flops 2 | bytes 131181 | solution.py:76
  326.7 39.9 %custom-call.38 = f32[4,128,128]{1,2,0:T(8,128)} custom-call(f32[4,128,128]{2,1,0:T(8,128)S(1)} %get-tuple-element.207), custom_call_target="InvertDiagBlocksLowerTriangular" | custom-call | tf_op jit(solution)/shard_map/triangular_solve/custom-call.3 | solution.py:76
  376.0 3.2 fusion.108
  379.3 4.1 convolution_subtract_fusion.1
  388.7 11.7 %cholesky.518 = f32[128,128]{1,0:T(8,128)S(1)} custom-call(f32[128,128]{1,0:T(8,128)S(1)} %cholesky.612), custom_call_target="Cholesky" | custom-call | tf_op jit(solution)/shard_map/jit(cholesky)/cholesky | solution.py:75
  401.1 10.8 %custom-call.39 = f32[1,128,128]{1,2,0:T(8,128)S(1)} custom-call(f32[1,128,128]{2,1,0:T(8,128)} %get-tuple-element.290), custom_call_target="InvertDiagBlocksLowerTriangular" | custom-call | tf_op jit(solution)/shard_map/jit(cholesky)/cholesky | solution.py:75
  417.9 4.0 fusion.223
  426.9 4.4 convolution_negate_fusion.2
  431.4 11.7 %cholesky.537 = f32[128,128]{1,0:T(8,128)S(1)} custom-call(f32[128,128]{1,0:T(8,128)S(1)} %slice-done), custom_call_target="Cholesky" | custom-call | tf_op jit(solution)/shard_map/jit(cholesky)/cholesky | solution.py:75
  445.3 10.0 %custom-call.40 = f32[1,128,128]{1,2,0:T(8,128)S(1)} custom-call(f32[1,128,128]{2,1,0:T(8,128)S(1)} %get-tuple-element.287), custom_call_target="InvertDiagBlocksLowerTriangular" | custom-call | tf_op jit(solution)/shard_map/jit(cholesky)/cholesky | solution.py:75
  458.4 13.2 %cholesky.558 = f32[128,128]{1,0:T(8,128)} custom-call(f32[128,128]{1,0:T(8,128)} %cholesky.621), custom_call_target="Cholesky" | custom-call | tf_op jit(solution)/shard_map/jit(cholesky)/cholesky | solution.py:75
  473.8 11.3 %custom-call.41 = f32[1,128,128]{1,2,0:T(8,128)} custom-call(f32[1,128,128]{2,1,0:T(8,128)} %get-tuple-element.284), custom_call_target="InvertDiagBlocksLowerTriangular" | custom-call | tf_op jit(solution)/shard_map/jit(cholesky)/cholesky | solution.py:75
  487.3 11.7 %cholesky.575 = f32[128,128]{1,0:T(8,128)S(1)} custom-call(f32[128,128]{1,0:T(8,128)S(1)} %convolution_subtract_fusion.17), custom_call_target="Cholesky" | custom-call | tf_op jit(solution)/shard_map/jit(cholesky)/cholesky | solution.py:75
  503.8 11.3 %while.24 = (s32[]{:T(128)}, f32[512,512]{1,0:T(8,128)}, s32[4,2]{0,1:T(2,128)S(1)}, f32[4,128,128]{2,1,0:T(8,128)S(1)}, s32[]{:T(128)}) while((s32[]{:T(128)}, f32[512,512]{1,0:T(8,128)}, s32[4,2]{0,1:T(2,128)S(1)}, f32[4,128,128]{2,1,0:T(8,128)S(1)}, s32[]{:T(128)}) %tuple.136), condition=%wide.while_cond.2.clone.1, body=%wide.while_body.2.clone.1.sunk | while | flops 2 | bytes 131181 | solution.py:76
  515.0 39.7 %custom-call.42 = f32[4,128,128]{1,2,0:T(8,128)S(1)} custom-call(f32[4,128,128]{2,1,0:T(8,128)S(1)} %get-tuple-element.208), custom_call_target="InvertDiagBlocksLowerTriangular" | custom-call | tf_op jit(solution)/shard_map/triangular_solve/custom-call.3 | solution.py:76
  562.5 3.5 convolution_add_fusion
  577.1 19.9 %fusion.38 = f32[1536,1536]{1,0:T(8,128)} fusion(f32[512,512]{1,0:T(8,128)S(1)} %cholesky.441, f32[512,512]{1,0:T(8,128)} %pad_maximum_fusion.1, f32[128,512]{1,0:T(8,128)} %copy-done.14, f32[128,512]{1,0:T(8,128)} %copy-done.12, f32[128,512]{1,0:T(8,128)S(1)} %fusion.243, f32[128,512]{1,0:T(8,128)S(1)} %fusion.205, f32[512,512]{1,0:T(8,128)} %convolution_negate_fusion, ...), kind=kLoop, calls=%fused_computation.76 | loop fusion | flops 33030144 | bytes 16777216 | tf_op jit(solution)/shard_map/concatenate | solution.py:127
  597.0 13.2 %fusion.140 = f32[96,1536]{1,0:T(8,128)S(1)} fusion(f32[1536,1536]{1,0:T(8,128)} %fusion.38, s32[1536]{0:T(1024)S(1)} %copy-done.30, s32[96]{0:T(128)S(1)} %sub.151, s32[1536]{0:T(1024)S(1)} %copy-done.28, s32[96]{0:T(128)S(1)} %sub.147, f32[1536]{0:T(1024)S(1)} %select_select_fusion.5, f32[96]{0:T(128)S(1)} %compare_select_fusion.1, ...), kind=kOutput, calls=%fused_computation.241 | convolution fusion | flops 2724249600 | bytes 10053120 | tf_op jit(solution)/shard_map/dot_general | solution.py:160
  614.8 4.8 stack.2
  619.7 10.2 %all-to-all-start = ((bf16[32,6,16,1536]{3,2,1,0:T(8,128)(2,1)}), bf16[32,6,16,1536]{3,2,1,0:T(8,128)(2,1)}, u32[]{:S(2)}, u32[]{:S(2)}) async-start(bf16[32,6,16,1536]{3,2,1,0:T(8,128)(2,1)} %stack.2), calls=%async_computation | async-start | bytes 18874368 | tf_op jit(solution)/shard_map/all_to_all | solution.py:18
  632.1 28.1 %fusion.79 = bf16[512,1536,1]{1,0,2:T(8,128)(2,1)S(1)} fusion(f32[1536,1536]{1,0:T(8,128)} %fusion.38, s32[1536]{0:T(1024)S(1)} %copy-done.30, s32[512]{0:T(512)S(1)} %dynamic_slice.42, s32[1536]{0:T(1024)S(1)} %copy-done.28, s32[512]{0:T(512)S(1)} %dynamic_slice.41, f32[1536]{0:T(1024)S(1)} %select_select_fusion.5, f32[512]{0:T(512)S(1)} %get-tuple-element.255, ...), kind=kOutput, calls=%fused_computation.131 | convolution fusion | flops 14530117632 | bytes 11042816 | tf_op jit(solution)/shard_map/dot_general | solution.py:189
  660.2 40.1 %while.21 = (s32[]{:T(128)}, f32[6,512,512]{2,1,0:T(8,128)}, s32[6]{0:T(128)S(1)}, s32[]{:T(128)}, s32[]{:T(128)}, /*index=5*/s32[6,512]{1,0:T(8,128)}, s32[512]...) while((s32[]{:T(128)}, f32[6,512,512]{2,1,0:T(8,128)}, ...), condition=%wide.region_9.12_spmd.clone, body=%wide.region_8.11_spmd.clone.sunk | while | flops 12324872 | bytes 1135325 | solution.py:187
  664.1 3.0 fusion.358
  700.4 141.9 %all-to-all-done = bf16[32,6,16,1536]{3,2,1,0:T(8,128)(2,1)} async-done(((bf16[32,6,16,1536]{3,2,1,0:T(8,128)(2,1)}), bf16[32,6,16,1536]{3,2,1,0:T(8,128)(2,1)}, u32[]{:S(2)}, u32[]{:S(2)}) %all-to-all-start) | async-done | bytes 9437216 | tf_op jit(solution)/shard_map/all_to_all | solution.py:18
  842.2 8.5 copy.58
  850.8 11.6 %convolution_subtract_fusion = f32[6,512,512]{2,1,0:T(8,128)} fusion(f32[6,512,512]{2,1,0:T(8,128)} %get-tuple-element.163, bf16[6,512,1536]{2,1,0:T(8,128)(2,1)} %bitcast.182, bf16[512,1536,1]{1,0,2:T(8,128)(2,1)S(1)} %fusion.79), kind=kOutput, calls=%fused_computation.132 | convolution fusion | flops 4833411072 | bytes 23592960 | tf_op jit(solution)/shard_map/sik,jk->sij/dot_general | solution.py:190
  (269 shorter events, 168.6 us)
Async XLA Ops:
  18.2 0.6 copy-start.24
  18.3 25.6 %copy-start.25 = (s32[1536]{0:T(1024)}, s32[1536]{0:T(1024)S(1)}, u32[]{:S(2)}) copy-start(s32[1536]{0:T(1024)S(1)} %slice.293) | copy-start | bytes 18436
  19.0 354.1 %copy-start.2 = (f32[512,512]{1,0:T(8,128)}, f32[512,512]{1,0:T(8,128)S(1)}, u32[]{:S(2)}) copy-start(f32[512,512]{1,0:T(8,128)S(1)} %fusion.116) | copy-start | bytes 3145732
  19.1 0.8 copy-start.31
  19.1 46.8 %copy-start.27 = (s32[1536]{0:T(1024)}, s32[1536]{0:T(1024)S(1)}, u32[]{:S(2)}) copy-start(s32[1536]{0:T(1024)S(1)} %slice.295) | copy-start | bytes 18436
  20.0 18.4 %copy-start.32 = (s32[24576]{0:T(1024)}, s32[24576]{0:T(1024)S(1)}, u32[]{:S(2)}) copy-start(s32[24576]{0:T(1024)S(1)} %reshape_squeeze.7) | copy-start | bytes 294916
  20.0 45.9 %copy-start.29 = (s32[1536]{0:T(1024)}, s32[1536]{0:T(1024)S(1)}, u32[]{:S(2)}) copy-start(s32[1536]{0:T(1024)S(1)} %slice.297) | copy-start | bytes 18436
  38.4 3.6 copy-start
  66.3 0.7 copy-start.22
  178.8 57.5 %copy-start.4 = (f32[128,512]{1,0:T(8,128)}, f32[128,512]{1,0:T(8,128)S(1)}, u32[]{:S(2)}) copy-start(f32[128,512]{1,0:T(8,128)S(1)} %fusion.209) | copy-start | bytes 786436
  179.7 7.2 copy-start.7
  180.5 6.3 copy-start.10
  181.6 5.3 copy-start.13
  199.0 2.0 copy-start.1
  206.4 1.0 copy-start.19
  370.4 5.7 copy-start.5
  373.1 6.2 copy-start.8
  376.0 3.2 copy-start.11
  387.7 1.0 copy-start.18
  417.9 13.6 %slice-start = ((f32[384,128]{1,0:T(8,128)}), f32[128,128]{1,0:T(8,128)S(1)}, s32[]{:S(2)}) async-start(f32[384,128]{1,0:T(8,128)} %convolution_subtract_fusion.11), calls=%async_computation.1 | async-start | bytes 131072 | tf_op jit(solution)/shard_map/jit(cholesky)/cholesky | solution.py:75
  426.9 127.8 %copy-start.3 = (f32[512,512]{1,0:T(8,128)S(1)}, f32[512,512]{1,0:T(8,128)}, u32[]{:S(2)}) copy-start(f32[512,512]{1,0:T(8,128)} %copy-done.2) | copy-start | bytes 3145732
  503.7 67.8 %copy-start.21 = (s32[2,6,512]{2,0,1:T(2,128)S(1)}, s32[2,6,512]{2,0,1:T(2,128)}, u32[]{:S(2)}) copy-start(s32[2,6,512]{2,0,1:T(2,128)} %param.11) | copy-start | bytes 73732
  554.8 2.1 copy-start.23
  554.8 13.1 %copy-start.15 = (f32[512,512]{1,0:T(8,128)S(1)}, f32[512,512]{1,0:T(8,128)}, u32[]{:S(2)}) copy-start(f32[512,512]{1,0:T(8,128)} %fusion.223) | copy-start | bytes 3145732
  558.2 18.9 %copy-start.6 = (f32[128,512]{1,0:T(8,128)S(1)}, f32[128,512]{1,0:T(8,128)}, u32[]{:S(2)}) copy-start(f32[128,512]{1,0:T(8,128)} %copy-done.5) | copy-start | bytes 786436
  558.2 18.9 %copy-start.9 = (f32[128,512]{1,0:T(8,128)S(1)}, f32[128,512]{1,0:T(8,128)}, u32[]{:S(2)}) copy-start(f32[128,512]{1,0:T(8,128)} %copy-done.8) | copy-start | bytes 786436
  559.6 8.3 copy-start.12
  562.5 14.5 %copy-start.14 = (f32[128,512]{1,0:T(8,128)}, f32[128,512]{1,0:T(8,128)S(1)}, u32[]{:S(2)}) copy-start(f32[128,512]{1,0:T(8,128)S(1)} %fusion.240) | copy-start | bytes 786436
  577.0 20.0 %copy-start.26 = (s32[1536]{0:T(1024)S(1)}, s32[1536]{0:T(1024)}, u32[]{:S(2)}) copy-start(s32[1536]{0:T(1024)} %copy-done.25) | copy-start | bytes 18436
  577.0 20.0 %copy-start.28 = (s32[1536]{0:T(1024)S(1)}, s32[1536]{0:T(1024)}, u32[]{:S(2)}) copy-start(s32[1536]{0:T(1024)} %copy-done.27) | copy-start | bytes 18436
  577.0 20.0 %copy-start.30 = (s32[1536]{0:T(1024)S(1)}, s32[1536]{0:T(1024)}, u32[]{:S(2)}) copy-start(s32[1536]{0:T(1024)} %copy-done.29) | copy-start | bytes 18436
  597.0 14.9 %copy-start.16 = (f32[512,512]{1,0:T(8,128)S(1)}, f32[512,512]{1,0:T(8,128)}, u32[]{:S(2)}) copy-start(f32[512,512]{1,0:T(8,128)} %get-tuple-element.264) | copy-start | bytes 3145732
  597.0 14.9 %copy-start.17 = (f32[512,512]{1,0:T(8,128)S(1)}, f32[512,512]{1,0:T(8,128)}, u32[]{:S(2)}) copy-start(f32[512,512]{1,0:T(8,128)} %get-tuple-element.262) | copy-start | bytes 3145732
  610.3 0.8 copy-start.20
  619.7 222.6 %all-to-all-start = ((bf16[32,6,16,1536]{3,2,1,0:T(8,128)(2,1)}), bf16[32,6,16,1536]{3,2,1,0:T(8,128)(2,1)}, u32[]{:S(2)}, u32[]{:S(2)}) async-start(bf16[32,6,16,1536]{3,2,1,0:T(8,128)(2,1)} %stack.2), calls=%async_computation | async-start | bytes 18874368 | tf_op jit(solution)/shard_map/all_to_all | solution.py:18
